TPU v7x, 128 devices: a whole 4x4x4 slice. The times are simulated.
128 devices in a mesh: view: 8 (over y_hi, x), gz: 16 (over z, y_lo, core).
Axes of the slice: x: 4, y: 4 (y_hi: 2, y_lo: 2; y = y_hi * 2 + y_lo), z: 4, core: 2. Of those that a mesh axis runs over, the one named last changes fastest.
Arguments:
- views_data: float32 [8, 256, 96, 1024], P('view', 'gz'), may hold values from 0.2 to 40
- estimate: float32 [256, 96, 1024], P('gz'), may hold values from 0.5 to 1.5
- kernels: float32 [8, 3, 31], P('view'), may hold values from 0.001 to 3
Outputs:
- deconvolved: float32 [256, 96, 1024], P('gz')
All inputs are finite; a program needn't handle non-finite values.
Results may differ from a plain program's by a relative error of at most 0.0001.
Values sent between devices are 32-bit elements; how exact they have to be, the bound alone decides.
No kernel may reach another device: no remote copies, remote signals or barrier semaphores. Data moves between devices by JAX's collectives and lax.ppermute only.
A program may use at most 128 MiB of HBM per device.

v0:
```python
import jax
import jax.numpy as jnp
from jax import lax
from jax.sharding import PartitionSpec as P

TAPS = 31
ITERS = 2
RADIUS = 15


def padded_2(value, sides, width):
    for axis, dim in sides:
        size, length = (lax.axis_size(axis), value.shape[dim])
        up = [(i, (i + 1) % size) for i in range(size - 1)]
        down = [(j, i) for i, j in up]
        last = lax.slice_in_dim(value, length - width, length, axis=dim)
        initial = lax.slice_in_dim(value, 0, width, axis=dim)
        before = lax.ppermute(last, axis, up)
        after = lax.ppermute(initial, axis, down)
        value = jnp.concatenate([before, value, after], axis=dim)
    return value


def toeplitz(tap_values, count):
    row_pos = jnp.arange(count)[:, None]
    col_pos = jnp.arange(count)[None, :]
    offsets = row_pos - col_pos + RADIUS
    matrix = jnp.zeros((count, count), jnp.float32)
    for offset in range(TAPS):
        matrix = matrix + jnp.where(offsets == offset, tap_values[offset], 0.0)
    return matrix


def tap_sum(padded, tap_values, flipped, depth):
    result = jnp.zeros((depth,) + padded.shape[1:], jnp.float32)
    for offset in range(TAPS):
        start = 2 * RADIUS - offset if flipped else offset
        result = result + tap_values[offset] * padded[start : start + depth]
    return result


def z_pass(volume, tap_values, flipped):
    padded = padded_2(volume, (("gz", 0),), RADIUS)
    return tap_sum(padded, tap_values, flipped, volume.shape[0])


def xy_pass(volume, mat_x, mat_y):
    passed = jnp.dot(volume, mat_x, precision=lax.Precision.HIGHEST)
    return jnp.einsum("zyx,yw->zwx", passed, mat_y, precision=lax.Precision.HIGHEST)


def per_device(views_data, estimate, kernels):
    tap_norm = kernels[0] / jnp.sum(kernels[0], axis=-1, keepdims=True)
    data_slab = views_data[0]
    mat_x = toeplitz(tap_norm[0], estimate.shape[2])
    mat_y = toeplitz(tap_norm[1], estimate.shape[1])
    views_count = lax.axis_size("view")
    for number in range(ITERS):
        blurred = z_pass(xy_pass(estimate, mat_x, mat_y), tap_norm[2], False)
        ratio = data_slab / blurred
        back = z_pass(xy_pass(ratio, mat_x.T, mat_y.T), tap_norm[2], True)
        logs = jnp.log(back)
        logsum = lax.psum(logs, "view")
        estimate = estimate * jnp.exp(logsum / views_count)
    return estimate


def solution(mesh):
    return jax.shard_map(
        per_device,
        mesh=mesh,
        in_specs=(P("view", "gz", None, None), P("gz", None, None), P("view", None, None)),
        out_specs=P("gz", None, None),
        check_vma=False,
    )
```

profile of v0, /device:TPU:1, one launch (start us, length us, event | category | flops | bytes accessed | tf_op | source)
XLA Modules:
  0.0 1528.6 jit_solution(3375969861306123260)
XLA Ops:
  6.5 0.0 all-reduce.3.cloned.1.call-start
  6.5 0.8 reduce_sum.9
  7.3 0.8 bitcast_divide_fusion
  8.1 0.7 fusion.832
  8.8 0.7 fusion.829
  9.5 0.7 fusion.831
  10.3 0.7 fusion.830
  11.0 45.9 %fusion.432 = f32[1024,16,96]{0,2,1:T(8,128)S(1)} fusion(f32[16,96,1024]{2,1,0:T(8,128)} %param.4, f32[]{:T(128)} %bitcast.65, f32[]{:T(128)} %bitcast.64, f32[]{:T(128)} %bitcast.63, f32[]{:T(128)} %bitcast.62, f32[]{:T(128)} %bitcast.61, f32[]{:T(128)} %bitcast.60, f32[]{:T(128)} %bitcast.59, f32[]{:T(128)} %bitcast.58, f32[]{:T(128)} %bitcast.57, ...), kind=kOutput, calls=%fused_computation.606 | convolution fusion | flops 19425918976 | bytes 12583036 | tf_op jit(solution)/shard_map/dot_general | solution.py:48
  56.9 26.1 %fusion.527 = f32[16,96,1024]{2,1,0:T(8,128)S(1)} fusion(f32[1024,16,96]{0,2,1:T(8,128)S(1)} %fusion.432, f32[]{:T(128)} %bitcast.31, f32[]{:T(128)} %bitcast.30, f32[]{:T(128)} %bitcast.29, f32[]{:T(128)} %bitcast.28, f32[]{:T(128)} %bitcast.27, f32[]{:T(128)} %bitcast.26, f32[]{:T(128)} %bitcast.25, f32[]{:T(128)} %bitcast.24, f32[]{:T(128)} %bitcast.23, ...), kind=kOutput, calls=%fused_computation.703 | convolution fusion | flops 1812805632 | bytes 12583036 | tf_op jit(solution)/shard_map/zyx,yw->zwx/dot_general | solution.py:49
  83.0 0.0 copy-start.1
  83.0 6.4 fusion.827
  89.4 0.0 copy-done.1
  89.4 4.6 collective-permute-start
  94.0 2.5 collective-permute-start.1
  96.5 0.7 fusion.828
  97.2 60.8 %collective-permute-done = f32[15,96,1024]{2,1,0:T(8,128)} collective-permute-done((f32[15,96,1024]{2,1,0:T(8,128)}, f32[15,96,1024]{2,1,0:T(8,128)}, u32[]{:S(2)}, u32[]{:S(2)}) %collective-permute-start) | collective-permute-done | bytes 5898272 | tf_op jit(solution)/shard_map/ppermute | solution.py:18
  158.0 65.2 %collective-permute-done.1 = f32[15,96,1024]{2,1,0:T(8,128)} collective-permute-done((f32[15,96,1024]{2,1,0:T(8,128)}, f32[15,96,1024]{2,1,0:T(8,128)}, u32[]{:S(2)}, u32[]{:S(2)}) %collective-permute-start.1) | collective-permute-done | bytes 5898272 | tf_op jit(solution)/shard_map/ppermute | solution.py:19
  223.1 153.6 %fusion.295 = f32[16,96,1024]{2,1,0:T(8,128)} fusion(f32[16,96,1024]{2,1,0:T(8,128)} %copy-done.1, f32[15,96,1024]{2,1,0:T(8,128)} %collective-permute-done.1, f32[15,96,1024]{2,1,0:T(8,128)} %collective-permute-done, f32[1,16,96,1024]{3,2,1,0:T(8,128)} %param.3, f32[]{:T(128)} %bitcast.98, f32[]{:T(128)} %bitcast.97, f32[]{:T(128)} %bitcast.96, ...), kind=kOutput, calls=%fused_computation.491 | convolution fusion | flops 19570622464 | bytes 30671096 | tf_op jit(solution)/shard_map/dot_general | solution.py:48
  376.7 27.5 %convolution_bitcast_fusion.2 = f32[16,96,1024]{2,1,0:T(8,128)S(1)} fusion(f32[16,96,1024]{2,1,0:T(8,128)} %fusion.295, f32[]{:T(128)} %bitcast.31, f32[]{:T(128)} %bitcast.30, f32[]{:T(128)} %bitcast.29, f32[]{:T(128)} %bitcast.28, f32[]{:T(128)} %bitcast.27, f32[]{:T(128)} %bitcast.26, f32[]{:T(128)} %bitcast.25, f32[]{:T(128)} %bitcast.24, ...), kind=kOutput, calls=%fused_computation.706 | convolution fusion | flops 1812805632 | bytes 12583036 | tf_op jit(solution)/shard_map/zyx,yw->zwx/dot_general | solution.py:49
  404.2 6.0 fusion.826
  410.2 2.1 collective-permute-start.2
  412.3 3.6 collective-permute-start.3
  415.9 121.8 %collective-permute-done.2 = f32[15,96,1024]{2,1,0:T(8,128)} collective-permute-done((f32[15,96,1024]{2,1,0:T(8,128)}, f32[15,96,1024]{2,1,0:T(8,128)}, u32[]{:S(2)}, u32[]{:S(2)}) %collective-permute-start.2) | collective-permute-done | bytes 5898272 | tf_op jit(solution)/shard_map/ppermute | solution.py:19
  537.7 0.0 collective-permute-done.3
  537.7 64.1 %fusion.207 = f32[16,96,1024]{2,1,0:T(8,128)} fusion(f32[16,96,1024]{2,1,0:T(8,128)S(1)} %convolution_bitcast_fusion.2, f32[15,96,1024]{2,1,0:T(8,128)} %collective-permute-done.3, f32[15,96,1024]{2,1,0:T(8,128)} %collective-permute-done.2, f32[]{:T(128)} %bitcast.98, f32[]{:T(128)} %bitcast.97, f32[]{:T(128)} %bitcast.96, f32[]{:T(128)} %bitcast.95, ...), kind=kLoop, calls=%fused_computation.403 | loop fusion | flops 143130624 | bytes 24379516 | tf_op jit(solution)/shard_map/log | solution.py:62
  601.8 0.0 all-reduce.3.cloned.1.call-update
  601.9 0.0 all-reduce.5.cloned.1.call-start
  601.9 152.4 %all-reduce.3.cloned.1.call-done = f32[16,96,1024]{2,1,0:T(8,128)} async-done(((f32[16,96,1024]{2,1,0:T(8,128)}), f32[16,96,1024]{2,1,0:T(8,128)}) %all-reduce.3.cloned.1.call-update) | async-done | bytes 6291472 | tf_op jit(solution)/shard_map/psum | solution.py:63
  754.3 66.6 %fusion.429 = f32[16,96,1024]{2,1,0:T(8,128)S(1)} fusion(f32[]{:T(128)} %bitcast.65, f32[]{:T(128)} %bitcast.64, f32[]{:T(128)} %bitcast.63, f32[]{:T(128)} %bitcast.62, f32[]{:T(128)} %bitcast.61, f32[]{:T(128)} %bitcast.60, f32[]{:T(128)} %bitcast.59, f32[]{:T(128)} %bitcast.58, f32[]{:T(128)} %bitcast.57, f32[]{:T(128)} %bitcast.56, f32[]{:T(128)} %bitcast.55, ...), kind=kOutput, calls=%fused_computation.603 | convolution fusion | flops 19429064704 | bytes 18874492 | tf_op jit(solution)/shard_map/dot_general | solution.py:48
  820.9 25.7 %convolution_bitcast_fusion.1 = f32[16,96,1024]{2,1,0:T(8,128)S(1)} fusion(f32[16,96,1024]{2,1,0:T(8,128)S(1)} %fusion.429, f32[]{:T(128)} %bitcast.31, f32[]{:T(128)} %bitcast.30, f32[]{:T(128)} %bitcast.29, f32[]{:T(128)} %bitcast.28, f32[]{:T(128)} %bitcast.27, f32[]{:T(128)} %bitcast.26, f32[]{:T(128)} %bitcast.25, f32[]{:T(128)} %bitcast.24, ...), kind=kOutput, calls=%fused_computation.705 | convolution fusion | flops 1812805632 | bytes 12583036 | tf_op jit(solution)/shard_map/zyx,yw->zwx/dot_general | solution.py:49
  846.6 0.0 copy-start
  846.7 6.4 fusion.825
  853.0 0.0 copy-done
  853.0 2.8 collective-permute-start.4
  855.8 4.0 collective-permute-start.5
  859.8 60.0 %collective-permute-done.4 = f32[15,96,1024]{2,1,0:T(8,128)} collective-permute-done((f32[15,96,1024]{2,1,0:T(8,128)}, f32[15,96,1024]{2,1,0:T(8,128)}, u32[]{:S(2)}, u32[]{:S(2)}) %collective-permute-start.4) | collective-permute-done | bytes 5898272 | tf_op jit(solution)/shard_map/ppermute | solution.py:18
  919.8 65.8 %collective-permute-done.5 = f32[15,96,1024]{2,1,0:T(8,128)} collective-permute-done((f32[15,96,1024]{2,1,0:T(8,128)}, f32[15,96,1024]{2,1,0:T(8,128)}, u32[]{:S(2)}, u32[]{:S(2)}) %collective-permute-start.5) | collective-permute-done | bytes 5898272 | tf_op jit(solution)/shard_map/ppermute | solution.py:19
  985.6 153.0 %fusion.92 = f32[16,96,1024]{2,1,0:T(8,128)} fusion(f32[16,96,1024]{2,1,0:T(8,128)} %copy-done, f32[15,96,1024]{2,1,0:T(8,128)} %collective-permute-done.5, f32[15,96,1024]{2,1,0:T(8,128)} %collective-permute-done.4, f32[1,16,96,1024]{3,2,1,0:T(8,128)} %param.3, f32[]{:T(128)} %bitcast.98, f32[]{:T(128)} %bitcast.97, f32[]{:T(128)} %bitcast.96, ...), kind=kOutput, calls=%fused_computation.316 | convolution fusion | flops 19570622464 | bytes 30671096 | tf_op jit(solution)/shard_map/dot_general | solution.py:48
  1138.6 27.5 %convolution_bitcast_fusion = f32[16,96,1024]{2,1,0:T(8,128)S(1)} fusion(f32[16,96,1024]{2,1,0:T(8,128)} %fusion.92, f32[]{:T(128)} %bitcast.31, f32[]{:T(128)} %bitcast.30, f32[]{:T(128)} %bitcast.29, f32[]{:T(128)} %bitcast.28, f32[]{:T(128)} %bitcast.27, f32[]{:T(128)} %bitcast.26, f32[]{:T(128)} %bitcast.25, f32[]{:T(128)} %bitcast.24, f32[]{:T(128)} %bitcast.23, ...), kind=kOutput, calls=%fused_computation.704 | convolution fusion | flops 1812805632 | bytes 12583036 | tf_op jit(solution)/shard_map/zyx,yw->zwx/dot_general | solution.py:49
  1166.1 6.0 fusion.824
  1172.0 2.2 collective-permute-start.6
  1174.2 3.6 collective-permute-start.7
  1177.9 122.6 %collective-permute-done.6 = f32[15,96,1024]{2,1,0:T(8,128)} collective-permute-done((f32[15,96,1024]{2,1,0:T(8,128)}, f32[15,96,1024]{2,1,0:T(8,128)}, u32[]{:S(2)}, u32[]{:S(2)}) %collective-permute-start.6) | collective-permute-done | bytes 5898272 | tf_op jit(solution)/shard_map/ppermute | solution.py:19
  1300.5 0.0 collective-permute-done.7
  1300.5 64.0 %fusion.4 = f32[16,96,1024]{2,1,0:T(8,128)} fusion(f32[16,96,1024]{2,1,0:T(8,128)S(1)} %convolution_bitcast_fusion, f32[15,96,1024]{2,1,0:T(8,128)} %collective-permute-done.7, f32[15,96,1024]{2,1,0:T(8,128)} %collective-permute-done.6, f32[]{:T(128)} %bitcast.98, f32[]{:T(128)} %bitcast.97, f32[]{:T(128)} %bitcast.96, f32[]{:T(128)} %bitcast.95, ...), kind=kLoop, calls=%fused_computation.228 | loop fusion | flops 143130624 | bytes 24379516 | tf_op jit(solution)/shard_map/log | solution.py:62
  1364.5 0.0 all-reduce.5.cloned.1.call-update
  1364.5 146.9 %all-reduce.5.cloned.1.call-done = f32[16,96,1024]{2,1,0:T(8,128)} async-done(((f32[16,96,1024]{2,1,0:T(8,128)}), f32[16,96,1024]{2,1,0:T(8,128)}) %all-reduce.5.cloned.1.call-update) | async-done | bytes 6291472 | tf_op jit(solution)/shard_map/psum | solution.py:63
  1511.4 9.9 exponential_multiply_fusion
Async XLA Ops:
  6.5 747.8 %all-reduce.3.cloned.1.call-start = ((), (), s32[]{:S(2)}) async-start(), calls=%async_computation | async-start | bytes 12582912 | tf_op jit(solution)/shard_map/psum | solution.py:63
  83.0 6.4 copy-start.1
  89.4 68.6 %collective-permute-start = (f32[15,96,1024]{2,1,0:T(8,128)}, f32[15,96,1024]{2,1,0:T(8,128)}, u32[]{:S(2)}, u32[]{:S(2)}) collective-permute-start(f32[15,96,1024]{2,1,0:T(8,128)} %get-tuple-element.11), channel_id=1, source_target_pairs={{0,1},{1,2},{2,3},{3,4},{4,5},{5,6},{6,7},{7,8},{8,9},{9,10},{10,1... | collective-permute-start | bytes 17694728 | tf_op jit(solution)/shard_map/ppermute | solution.py:18
  94.0 129.2 %collective-permute-start.1 = (f32[15,96,1024]{2,1,0:T(8,128)}, f32[15,96,1024]{2,1,0:T(8,128)}, u32[]{:S(2)}, u32[]{:S(2)}) collective-permute-start(f32[15,96,1024]{2,1,0:T(8,128)} %get-tuple-element.12), channel_id=1, source_target_pairs={{1,0},{2,1},{3,2},{4,3},{5,4},{6,5},{7,6},{8,7},{9,8},{10,9},{11,1... | collective-permute-start | bytes 17694728 | tf_op jit(solution)/shard_map/ppermute | solution.py:19
  410.2 127.5 %collective-permute-start.2 = (f32[15,96,1024]{2,1,0:T(8,128)}, f32[15,96,1024]{2,1,0:T(8,128)}, u32[]{:S(2)}, u32[]{:S(2)}) collective-permute-start(f32[15,96,1024]{2,1,0:T(8,128)} %get-tuple-element.9), channel_id=1, source_target_pairs={{1,0},{2,1},{3,2},{4,3},{5,4},{6,5},{7,6},{8,7},{9,8},{10,9},{11,1... | collective-permute-start | bytes 17694728 | tf_op jit(solution)/shard_map/ppermute | solution.py:19
  412.3 125.4 %collective-permute-start.3 = (f32[15,96,1024]{2,1,0:T(8,128)}, f32[15,96,1024]{2,1,0:T(8,128)}, u32[]{:S(2)}, u32[]{:S(2)}) collective-permute-start(f32[15,96,1024]{2,1,0:T(8,128)} %get-tuple-element.10), channel_id=1, source_target_pairs={{0,1},{1,2},{2,3},{3,4},{4,5},{5,6},{6,7},{7,8},{8,9},{9,10},{10,1... | collective-permute-start | bytes 17694728 | tf_op jit(solution)/shard_map/ppermute | solution.py:18
  601.9 909.5 %all-reduce.5.cloned.1.call-start = ((), (), s32[]{:S(2)}) async-start(), calls=%async_computation.1 | async-start | bytes 12582912 | tf_op jit(solution)/shard_map/psum | solution.py:63
  846.6 6.4 copy-start
  853.0 66.8 %collective-permute-start.4 = (f32[15,96,1024]{2,1,0:T(8,128)}, f32[15,96,1024]{2,1,0:T(8,128)}, u32[]{:S(2)}, u32[]{:S(2)}) collective-permute-start(f32[15,96,1024]{2,1,0:T(8,128)} %get-tuple-element.7), channel_id=1, source_target_pairs={{0,1},{1,2},{2,3},{3,4},{4,5},{5,6},{6,7},{7,8},{8,9},{9,10},{10,1... | collective-permute-start | bytes 17694728 | tf_op jit(solution)/shard_map/ppermute | solution.py:18
  855.8 129.8 %collective-permute-start.5 = (f32[15,96,1024]{2,1,0:T(8,128)}, f32[15,96,1024]{2,1,0:T(8,128)}, u32[]{:S(2)}, u32[]{:S(2)}) collective-permute-start(f32[15,96,1024]{2,1,0:T(8,128)} %get-tuple-element.8), channel_id=1, source_target_pairs={{1,0},{2,1},{3,2},{4,3},{5,4},{6,5},{7,6},{8,7},{9,8},{10,9},{11,1... | collective-permute-start | bytes 17694728 | tf_op jit(solution)/shard_map/ppermute | solution.py:19
  1172.0 128.4 %collective-permute-start.6 = (f32[15,96,1024]{2,1,0:T(8,128)}, f32[15,96,1024]{2,1,0:T(8,128)}, u32[]{:S(2)}, u32[]{:S(2)}) collective-permute-start(f32[15,96,1024]{2,1,0:T(8,128)} %get-tuple-element.5), channel_id=1, source_target_pairs={{1,0},{2,1},{3,2},{4,3},{5,4},{6,5},{7,6},{8,7},{9,8},{10,9},{11,1... | collective-permute-start | bytes 17694728 | tf_op jit(solution)/shard_map/ppermute | solution.py:19
  1174.2 126.3 %collective-permute-start.7 = (f32[15,96,1024]{2,1,0:T(8,128)}, f32[15,96,1024]{2,1,0:T(8,128)}, u32[]{:S(2)}, u32[]{:S(2)}) collective-permute-start(f32[15,96,1024]{2,1,0:T(8,128)} %get-tuple-element.6), channel_id=1, source_target_pairs={{0,1},{1,2},{2,3},{3,4},{4,5},{5,6},{6,7},{7,8},{8,9},{9,10},{10,1... | collective-permute-start | bytes 17694728 | tf_op jit(solution)/shard_map/ppermute | solution.py:18
Sparse Core Ops, SparseCore 0:
  602.0 152.2 all-reduce.2
  1364.6 146.7 all-reduce.4
where the time goes:
time: 1540 us; the launch traced here: 1530 us
  waiting for transfers between devices  795 us (52%)
  matrix products  526 us (34%)
  other arithmetic  140 us (9%)
  local copies, waits for them, and re-layouts  28.3 us (2%)
  starting transfers between devices  25.4 us (2%)
    dot_general x4, matrix products, xy_pass(): passed = jnp.dot(volume, mat_x, precision=lax.Precision.HIGHEST)  419 us
    ppermute x4, waiting for transfers between devices, padded_2(): after = lax.ppermute(initial, axis, down)  375 us
    psum x2, waiting for transfers between devices, per_device(): logsum = lax.psum(logs, 'view')  299 us
    log x2, other arithmetic, per_device(): logs = jnp.log(back)  128 us
    ppermute x4, waiting for transfers between devices, padded_2(): before = lax.ppermute(last, axis, up)  121 us
    dot_general x4, matrix products, xy_pass(): jnp.einsum('zyx,yw->zwx', passed, mat_y, precision=lax.Precision.HIGHEST)  107 us
  transfers between devices with their start and end apart: 10, of which 8 were waited for; matrix products, arithmetic and copies ran while one was open for 0% of the time, Pallas kernels for 0%

commit v1 on v0

--- a/solution.py
+++ b/solution.py
@@ -60,7 +60,8 @@
         ratio = data_slab / blurred
         back = z_pass(xy_pass(ratio, mat_x.T, mat_y.T), tap_norm[2], True)
         logs = jnp.log(back)
-        logsum = lax.psum(logs, "view")
+        parts = lax.all_gather(logs, "view", axis=0, tiled=False)
+        logsum = parts.sum(axis=0)
         estimate = estimate * jnp.exp(logsum / views_count)
     return estimate
 

time: 1540 us -> 2270 us (1.47)
  waiting for transfers between devices: 795 us -> 1490 us
  other arithmetic: 140 us -> 180 us
    all_gather x0 -> x2, waiting for transfers between devices: none -> 996 us  [per_device(): parts = lax.all_gather(logs, 'view', axis=0, tiled=False)]
    psum x2 -> x0, waiting for transfers between devices: 299 us -> none  [per_device(): logsum = lax.psum(logs, 'view')]
    reduce_sum x0 -> x2, other arithmetic: none -> 42.2 us  [per_device(): logsum = parts.sum(axis=0)]
where the time goes in v1:
time: 2270 us; the launch traced here: 2260 us
  waiting for transfers between devices  1490 us (66%)
  matrix products  520 us (23%)
  other arithmetic  180 us (8%)
  local copies, waits for them, and re-layouts  27.9 us (1%)
  starting transfers between devices  25.4 us (1%)
    all_gather x2, waiting for transfers between devices, per_device(): parts = lax.all_gather(logs, 'view', axis=0, tiled=False)  996 us
    dot_general x4, matrix products, xy_pass(): passed = jnp.dot(volume, mat_x, precision=lax.Precision.HIGHEST)  413 us
    ppermute x4, waiting for transfers between devices, padded_2(): after = lax.ppermute(initial, axis, down)  375 us
    log x2, other arithmetic, per_device(): logs = jnp.log(back)  126 us
    ppermute x4, waiting for transfers between devices, padded_2(): before = lax.ppermute(last, axis, up)  121 us
    dot_general x4, matrix products, xy_pass(): jnp.einsum('zyx,yw->zwx', passed, mat_y, precision=lax.Precision.HIGHEST)  108 us
  transfers between devices with their start and end apart: 10, of which 8 were waited for; matrix products, arithmetic and copies ran while one was open for 0% of the time, Pallas kernels for 0%

profile of v1, /device:TPU:1, one launch (start us, length us, event | category | flops | bytes accessed | tf_op | source)
XLA Modules:
  0.0 2259.3 jit_solution(6561220825755036773)
XLA Ops:
  6.5 0.0 all-gather.5.cloned.1.call-start
  6.5 0.8 reduce_sum.27
  7.3 0.8 bitcast_divide_fusion
  8.1 0.7 fusion.832
  8.8 0.7 fusion.829
  9.5 0.7 fusion.831
  10.3 0.7 fusion.830
  11.0 45.1 %fusion.432 = f32[1024,16,96]{0,2,1:T(8,128)S(1)} fusion(f32[16,96,1024]{2,1,0:T(8,128)} %param.4, f32[]{:T(128)} %bitcast.65, f32[]{:T(128)} %bitcast.64, f32[]{:T(128)} %bitcast.63, f32[]{:T(128)} %bitcast.62, f32[]{:T(128)} %bitcast.61, f32[]{:T(128)} %bitcast.60, f32[]{:T(128)} %bitcast.59, f32[]{:T(128)} %bitcast.58, f32[]{:T(128)} %bitcast.57, ...), kind=kOutput, calls=%fused_computation.606 | convolution fusion | flops 19425918976 | bytes 12583036 | tf_op jit(solution)/shard_map/dot_general | solution.py:48
  56.1 26.3 %fusion.527 = f32[16,96,1024]{2,1,0:T(8,128)S(1)} fusion(f32[1024,16,96]{0,2,1:T(8,128)S(1)} %fusion.432, f32[]{:T(128)} %bitcast.31, f32[]{:T(128)} %bitcast.30, f32[]{:T(128)} %bitcast.29, f32[]{:T(128)} %bitcast.28, f32[]{:T(128)} %bitcast.27, f32[]{:T(128)} %bitcast.26, f32[]{:T(128)} %bitcast.25, f32[]{:T(128)} %bitcast.24, f32[]{:T(128)} %bitcast.23, ...), kind=kOutput, calls=%fused_computation.703 | convolution fusion | flops 1812805632 | bytes 12583036 | tf_op jit(solution)/shard_map/zyx,yw->zwx/dot_general | solution.py:49
  82.4 0.0 copy-start.1
  82.4 6.4 fusion.827
  88.8 4.6 collective-permute-start
  93.4 2.5 collective-permute-start.1
  95.9 0.7 fusion.828
  96.6 60.8 %collective-permute-done = f32[15,96,1024]{2,1,0:T(8,128)} collective-permute-done((f32[15,96,1024]{2,1,0:T(8,128)}, f32[15,96,1024]{2,1,0:T(8,128)}, u32[]{:S(2)}, u32[]{:S(2)}) %collective-permute-start) | collective-permute-done | bytes 5898272 | tf_op jit(solution)/shard_map/ppermute | solution.py:18
  157.4 65.2 %collective-permute-done.1 = f32[15,96,1024]{2,1,0:T(8,128)} collective-permute-done((f32[15,96,1024]{2,1,0:T(8,128)}, f32[15,96,1024]{2,1,0:T(8,128)}, u32[]{:S(2)}, u32[]{:S(2)}) %collective-permute-start.1) | collective-permute-done | bytes 5898272 | tf_op jit(solution)/shard_map/ppermute | solution.py:19
  222.5 151.4 %fusion.295 = f32[16,96,1024]{2,1,0:T(8,128)} fusion(f32[16,96,1024]{2,1,0:T(8,128)} %copy-done.1, f32[15,96,1024]{2,1,0:T(8,128)} %collective-permute-done.1, f32[15,96,1024]{2,1,0:T(8,128)} %collective-permute-done, f32[1,16,96,1024]{3,2,1,0:T(8,128)} %param.3, f32[]{:T(128)} %bitcast.98, f32[]{:T(128)} %bitcast.97, f32[]{:T(128)} %bitcast.96, ...), kind=kOutput, calls=%fused_computation.491 | convolution fusion | flops 19570622464 | bytes 30671096 | tf_op jit(solution)/shard_map/dot_general | solution.py:48
  374.0 27.7 %convolution_bitcast_fusion.2 = f32[16,96,1024]{2,1,0:T(8,128)S(1)} fusion(f32[16,96,1024]{2,1,0:T(8,128)} %fusion.295, f32[]{:T(128)} %bitcast.31, f32[]{:T(128)} %bitcast.30, f32[]{:T(128)} %bitcast.29, f32[]{:T(128)} %bitcast.28, f32[]{:T(128)} %bitcast.27, f32[]{:T(128)} %bitcast.26, f32[]{:T(128)} %bitcast.25, f32[]{:T(128)} %bitcast.24, ...), kind=kOutput, calls=%fused_computation.706 | convolution fusion | flops 1812805632 | bytes 12583036 | tf_op jit(solution)/shard_map/zyx,yw->zwx/dot_general | solution.py:49
  401.6 6.0 fusion.826
  407.6 2.1 collective-permute-start.2
  409.7 3.6 collective-permute-start.3
  413.4 121.8 %collective-permute-done.2 = f32[15,96,1024]{2,1,0:T(8,128)} collective-permute-done((f32[15,96,1024]{2,1,0:T(8,128)}, f32[15,96,1024]{2,1,0:T(8,128)}, u32[]{:S(2)}, u32[]{:S(2)}) %collective-permute-start.2) | collective-permute-done | bytes 5898272 | tf_op jit(solution)/shard_map/ppermute | solution.py:19
  535.1 0.0 collective-permute-done.3
  535.1 63.1 %fusion.207 = f32[16,96,1024]{2,1,0:T(8,128)} fusion(f32[16,96,1024]{2,1,0:T(8,128)S(1)} %convolution_bitcast_fusion.2, f32[15,96,1024]{2,1,0:T(8,128)} %collective-permute-done.3, f32[15,96,1024]{2,1,0:T(8,128)} %collective-permute-done.2, f32[]{:T(128)} %bitcast.98, f32[]{:T(128)} %bitcast.97, f32[]{:T(128)} %bitcast.96, f32[]{:T(128)} %bitcast.95, ...), kind=kLoop, calls=%fused_computation.403 | loop fusion | flops 143130624 | bytes 24379516 | tf_op jit(solution)/shard_map/log | solution.py:62
  598.2 0.0 all-gather.5.cloned.1.call-update
  598.3 0.0 all-gather.7.cloned.1.call-start
  598.3 500.2 %all-gather.5.cloned.1.call-done = f32[128,96,1024]{2,1,0:T(8,128)} async-done(((f32[16,96,1024]{2,1,0:T(8,128)}), f32[128,96,1024]{2,1,0:T(8,128)}) %all-gather.5.cloned.1.call-update) | async-done | bytes 50331664 | tf_op jit(solution)/shard_map/all_gather | solution.py:63
  1098.6 21.2 reduce_sum.28
  1119.7 65.8 %fusion.429 = f32[16,96,1024]{2,1,0:T(8,128)S(1)} fusion(f32[]{:T(128)} %bitcast.65, f32[]{:T(128)} %bitcast.64, f32[]{:T(128)} %bitcast.63, f32[]{:T(128)} %bitcast.62, f32[]{:T(128)} %bitcast.61, f32[]{:T(128)} %bitcast.60, f32[]{:T(128)} %bitcast.59, f32[]{:T(128)} %bitcast.58, f32[]{:T(128)} %bitcast.57, f32[]{:T(128)} %bitcast.56, f32[]{:T(128)} %bitcast.55, ...), kind=kOutput, calls=%fused_computation.603 | convolution fusion | flops 19429064704 | bytes 18874492 | tf_op jit(solution)/shard_map/dot_general | solution.py:48
  1185.6 25.9 %convolution_bitcast_fusion.1 = f32[16,96,1024]{2,1,0:T(8,128)S(1)} fusion(f32[16,96,1024]{2,1,0:T(8,128)S(1)} %fusion.429, f32[]{:T(128)} %bitcast.31, f32[]{:T(128)} %bitcast.30, f32[]{:T(128)} %bitcast.29, f32[]{:T(128)} %bitcast.28, f32[]{:T(128)} %bitcast.27, f32[]{:T(128)} %bitcast.26, f32[]{:T(128)} %bitcast.25, f32[]{:T(128)} %bitcast.24, ...), kind=kOutput, calls=%fused_computation.705 | convolution fusion | flops 1812805632 | bytes 12583036 | tf_op jit(solution)/shard_map/zyx,yw->zwx/dot_general | solution.py:49
  1211.5 0.0 copy-start
  1211.5 6.2 fusion.825
  1217.6 3.2 collective-permute-start.4
  1220.8 3.6 collective-permute-start.5
  1224.4 60.4 %collective-permute-done.4 = f32[15,96,1024]{2,1,0:T(8,128)} collective-permute-done((f32[15,96,1024]{2,1,0:T(8,128)}, f32[15,96,1024]{2,1,0:T(8,128)}, u32[]{:S(2)}, u32[]{:S(2)}) %collective-permute-start.4) | collective-permute-done | bytes 5898272 | tf_op jit(solution)/shard_map/ppermute | solution.py:18
  1284.8 65.8 %collective-permute-done.5 = f32[15,96,1024]{2,1,0:T(8,128)} collective-permute-done((f32[15,96,1024]{2,1,0:T(8,128)}, f32[15,96,1024]{2,1,0:T(8,128)}, u32[]{:S(2)}, u32[]{:S(2)}) %collective-permute-start.5) | collective-permute-done | bytes 5898272 | tf_op jit(solution)/shard_map/ppermute | solution.py:19
  1350.6 150.2 %fusion.92 = f32[16,96,1024]{2,1,0:T(8,128)} fusion(f32[16,96,1024]{2,1,0:T(8,128)} %copy-done, f32[15,96,1024]{2,1,0:T(8,128)} %collective-permute-done.5, f32[15,96,1024]{2,1,0:T(8,128)} %collective-permute-done.4, f32[1,16,96,1024]{3,2,1,0:T(8,128)} %param.3, f32[]{:T(128)} %bitcast.98, f32[]{:T(128)} %bitcast.97, f32[]{:T(128)} %bitcast.96, ...), kind=kOutput, calls=%fused_computation.316 | convolution fusion | flops 19570622464 | bytes 30671096 | tf_op jit(solution)/shard_map/dot_general | solution.py:48
  1500.8 27.7 %convolution_bitcast_fusion = f32[16,96,1024]{2,1,0:T(8,128)S(1)} fusion(f32[16,96,1024]{2,1,0:T(8,128)} %fusion.92, f32[]{:T(128)} %bitcast.31, f32[]{:T(128)} %bitcast.30, f32[]{:T(128)} %bitcast.29, f32[]{:T(128)} %bitcast.28, f32[]{:T(128)} %bitcast.27, f32[]{:T(128)} %bitcast.26, f32[]{:T(128)} %bitcast.25, f32[]{:T(128)} %bitcast.24, f32[]{:T(128)} %bitcast.23, ...), kind=kOutput, calls=%fused_computation.704 | convolution fusion | flops 1812805632 | bytes 12583036 | tf_op jit(solution)/shard_map/zyx,yw->zwx/dot_general | solution.py:49
  1528.5 5.8 fusion.824
  1534.3 2.2 collective-permute-start.6
  1536.5 3.6 collective-permute-start.7
  1540.2 122.6 %collective-permute-done.6 = f32[15,96,1024]{2,1,0:T(8,128)} collective-permute-done((f32[15,96,1024]{2,1,0:T(8,128)}, f32[15,96,1024]{2,1,0:T(8,128)}, u32[]{:S(2)}, u32[]{:S(2)}) %collective-permute-start.6) | collective-permute-done | bytes 5898272 | tf_op jit(solution)/shard_map/ppermute | solution.py:19
  1662.8 0.0 collective-permute-done.7
  1662.8 62.9 %fusion.4 = f32[16,96,1024]{2,1,0:T(8,128)} fusion(f32[16,96,1024]{2,1,0:T(8,128)S(1)} %convolution_bitcast_fusion, f32[15,96,1024]{2,1,0:T(8,128)} %collective-permute-done.7, f32[15,96,1024]{2,1,0:T(8,128)} %collective-permute-done.6, f32[]{:T(128)} %bitcast.98, f32[]{:T(128)} %bitcast.97, f32[]{:T(128)} %bitcast.96, f32[]{:T(128)} %bitcast.95, ...), kind=kLoop, calls=%fused_computation.228 | loop fusion | flops 143130624 | bytes 24379516 | tf_op jit(solution)/shard_map/log | solution.py:62
  1725.7 0.0 all-gather.7.cloned.1.call-update
  1725.7 495.3 %all-gather.7.cloned.1.call-done = f32[128,96,1024]{2,1,0:T(8,128)} async-done(((f32[16,96,1024]{2,1,0:T(8,128)}), f32[128,96,1024]{2,1,0:T(8,128)}) %all-gather.7.cloned.1.call-update) | async-done | bytes 50331664 | tf_op jit(solution)/shard_map/all_gather | solution.py:63
  2221.0 21.1 reduce_sum.29
  2242.1 9.9 exponential_multiply_fusion
  (2 shorter events, 0.0 us)
Async XLA Ops:
  6.5 1092.0 %all-gather.5.cloned.1.call-start = ((), (), s32[]{:S(2)}) async-start(), calls=%async_computation | async-start | bytes 56623104 | tf_op jit(solution)/shard_map/all_gather | solution.py:63
  82.4 6.4 copy-start.1
  88.8 68.6 %collective-permute-start = (f32[15,96,1024]{2,1,0:T(8,128)}, f32[15,96,1024]{2,1,0:T(8,128)}, u32[]{:S(2)}, u32[]{:S(2)}) collective-permute-start(f32[15,96,1024]{2,1,0:T(8,128)} %get-tuple-element.11), channel_id=1, source_target_pairs={{0,1},{1,2},{2,3},{3,4},{4,5},{5,6},{6,7},{7,8},{8,9},{9,10},{10,1... | collective-permute-start | bytes 17694728 | tf_op jit(solution)/shard_map/ppermute | solution.py:18
  93.4 129.2 %collective-permute-start.1 = (f32[15,96,1024]{2,1,0:T(8,128)}, f32[15,96,1024]{2,1,0:T(8,128)}, u32[]{:S(2)}, u32[]{:S(2)}) collective-permute-start(f32[15,96,1024]{2,1,0:T(8,128)} %get-tuple-element.12), channel_id=1, source_target_pairs={{1,0},{2,1},{3,2},{4,3},{5,4},{6,5},{7,6},{8,7},{9,8},{10,9},{11,1... | collective-permute-start | bytes 17694728 | tf_op jit(solution)/shard_map/ppermute | solution.py:19
  407.6 127.5 %collective-permute-start.2 = (f32[15,96,1024]{2,1,0:T(8,128)}, f32[15,96,1024]{2,1,0:T(8,128)}, u32[]{:S(2)}, u32[]{:S(2)}) collective-permute-start(f32[15,96,1024]{2,1,0:T(8,128)} %get-tuple-element.9), channel_id=1, source_target_pairs={{1,0},{2,1},{3,2},{4,3},{5,4},{6,5},{7,6},{8,7},{9,8},{10,9},{11,1... | collective-permute-start | bytes 17694728 | tf_op jit(solution)/shard_map/ppermute | solution.py:19
  409.7 125.4 %collective-permute-start.3 = (f32[15,96,1024]{2,1,0:T(8,128)}, f32[15,96,1024]{2,1,0:T(8,128)}, u32[]{:S(2)}, u32[]{:S(2)}) collective-permute-start(f32[15,96,1024]{2,1,0:T(8,128)} %get-tuple-element.10), channel_id=1, source_target_pairs={{0,1},{1,2},{2,3},{3,4},{4,5},{5,6},{6,7},{7,8},{8,9},{9,10},{10,1... | collective-permute-start | bytes 17694728 | tf_op jit(solution)/shard_map/ppermute | solution.py:18
  598.3 1622.8 %all-gather.7.cloned.1.call-start = ((), (), s32[]{:S(2)}) async-start(), calls=%async_computation.1 | async-start | bytes 56623104 | tf_op jit(solution)/shard_map/all_gather | solution.py:63
  1211.5 6.2 copy-start
  1217.6 67.2 %collective-permute-start.4 = (f32[15,96,1024]{2,1,0:T(8,128)}, f32[15,96,1024]{2,1,0:T(8,128)}, u32[]{:S(2)}, u32[]{:S(2)}) collective-permute-start(f32[15,96,1024]{2,1,0:T(8,128)} %get-tuple-element.7), channel_id=1, source_target_pairs={{0,1},{1,2},{2,3},{3,4},{4,5},{5,6},{6,7},{7,8},{8,9},{9,10},{10,1... | collective-permute-start | bytes 17694728 | tf_op jit(solution)/shard_map/ppermute | solution.py:18
  1220.8 129.8 %collective-permute-start.5 = (f32[15,96,1024]{2,1,0:T(8,128)}, f32[15,96,1024]{2,1,0:T(8,128)}, u32[]{:S(2)}, u32[]{:S(2)}) collective-permute-start(f32[15,96,1024]{2,1,0:T(8,128)} %get-tuple-element.8), channel_id=1, source_target_pairs={{1,0},{2,1},{3,2},{4,3},{5,4},{6,5},{7,6},{8,7},{9,8},{10,9},{11,1... | collective-permute-start | bytes 17694728 | tf_op jit(solution)/shard_map/ppermute | solution.py:19
  1534.3 128.4 %collective-permute-start.6 = (f32[15,96,1024]{2,1,0:T(8,128)}, f32[15,96,1024]{2,1,0:T(8,128)}, u32[]{:S(2)}, u32[]{:S(2)}) collective-permute-start(f32[15,96,1024]{2,1,0:T(8,128)} %get-tuple-element.5), channel_id=1, source_target_pairs={{1,0},{2,1},{3,2},{4,3},{5,4},{6,5},{7,6},{8,7},{9,8},{10,9},{11,1... | collective-permute-start | bytes 17694728 | tf_op jit(solution)/shard_map/ppermute | solution.py:19
  1536.5 126.3 %collective-permute-start.7 = (f32[15,96,1024]{2,1,0:T(8,128)}, f32[15,96,1024]{2,1,0:T(8,128)}, u32[]{:S(2)}, u32[]{:S(2)}) collective-permute-start(f32[15,96,1024]{2,1,0:T(8,128)} %get-tuple-element.6), channel_id=1, source_target_pairs={{0,1},{1,2},{2,3},{3,4},{4,5},{5,6},{6,7},{7,8},{8,9},{9,10},{10,1... | collective-permute-start | bytes 17694728 | tf_op jit(solution)/shard_map/ppermute | solution.py:18
Sparse Core Ops, SparseCore 0:
  598.4 500.1 all-gather.4
  1725.9 495.1 all-gather.6
